TPU v7x, 512 devices: a whole 4x8x8 slice. The times are simulated.
512 devices in a mesh: img: 16 (over x, y_lo, core), vol: 32 (over z, y_hi).
Axes of the slice: x: 4, y: 8 (y_hi: 4, y_lo: 2; y = y_hi * 2 + y_lo), z: 8, core: 2. Of those that a mesh axis runs over, the one named last changes fastest.
Arguments:
- volume: float32 [512, 16, 4, 256], P('vol', 'img'), may hold values from -6 to 6
- images: bfloat16 [16384, 8, 256], P(('img', 'vol')), may hold values from -6 to 6
- ctf: float32 [16384, 8, 128], P(('img', 'vol')), may hold values from -1 to 1
- noise_weight: float32 [16384, 8, 128], P(('img', 'vol')), may hold values from 0.025 to 8, as said below
- shifts: float32 [16384, 2, 32], P(('img', 'vol')), may hold values from -4 to 4
- orient: int32 [16384, 64], P(('img', 'vol')), may hold values from 0 to 191, all different within a row
- counts: int32 [16384], P(('img', 'vol')), may hold values from 1 to 64
- tile_map: int32 [192, 8, 8], replicated, may hold values from 0 to 32767
- interp: float32 [192, 8, 8], replicated, may hold values from 0.05 to 0.3
Outputs:
- real_space: float32 [2, 512, 16, 512], P(None, None, 'img', 'vol')
- evidence: float32 [16384], P(('img', 'vol'))
Inputs may be any that keep to these rules, and one draw needn't show every extreme that they name: `orient`: the 64 entries of one image are different orientations. `noise_weight`: positive.
All inputs are finite; a program needn't handle non-finite values.
Results may differ from a plain program's by a relative error of at most 0.0068.
Values may be sent and summed in bfloat16 or wider, within the bound.
No kernel may reach another device: no remote copies, remote signals or barrier semaphores. Data moves between devices by JAX's collectives and lax.ppermute only.
A program may use at most 64 MiB of HBM per device.

v0:
```python
import functools
import math

import jax
import jax.numpy as jnp
from jax import lax
from jax.experimental import pallas as pl
from jax.experimental.pallas import tpu as pltpu
from jax.sharding import PartitionSpec as P

BOX = 256
f32 = jnp.float32
bf16 = jnp.bfloat16
precise = lax.Precision.HIGHEST
LOWEST = -3.0e38


def cos_sin_turns(turns):
    u = (turns - jnp.round(turns)) * (-math.pi)
    v = u * u
    s = 1.0 / 6227020800.0
    for coefficient in (-39916800.0, 362880.0, -5040.0, 120.0, -6.0, 1.0):
        s = s * v + 1.0 / coefficient
    s = s * u
    c = 1.0 / 479001600.0
    for coefficient in (-3628800.0, 40320.0, -720.0, 24.0, -2.0, 1.0):
        c = c * v + 1.0 / coefficient
    return 1.0 - 2.0 * s * s, 2.0 * s * c


def weighted_kernel(images_ref, ctf_ref, noise_ref, shift_ref, out_ref):
    num_images, rows_per, tile_len = ctf_ref.shape
    trials = shift_ref.shape[0] // num_images

    def one_image(index, carry):
        base = pl.multiple_of(index * trials, trials)
        rows = pl.ds(base, trials)
        column = lax.broadcasted_iota(jnp.int32, (trials, tile_len), 1).astype(f32) * (1.0 / BOX)
        shift_x = jnp.broadcast_to(shift_ref[rows, 0:1], (trials, tile_len))
        shift_y = jnp.broadcast_to(shift_ref[rows, 1:2], (trials, tile_len))
        cosine, sine = cos_sin_turns(shift_x * column)
        step_cos, step_sin = cos_sin_turns(shift_y * (1.0 / BOX))
        image = images_ref[index].astype(f32)
        factor = ctf_ref[index] * noise_ref[index]
        real = image[:, :tile_len] * factor
        imag = image[:, tile_len:] * factor
        for p in range(rows_per):
            re = jnp.broadcast_to(real[p : p + 1, :], (trials, tile_len))
            im = jnp.broadcast_to(imag[p : p + 1, :], (trials, tile_len))
            out_ref[p, rows, :tile_len] = (re * cosine - im * sine).astype(bf16)
            out_ref[p, rows, tile_len:] = (re * sine + im * cosine).astype(bf16)
            if p + 1 < rows_per:
                cosine, sine = (
                    cosine * step_cos - sine * step_sin,
                    sine * step_cos + cosine * step_sin,
                )
        return carry

    lax.fori_loop(0, num_images, one_image, 0)


def expectation_kernel(
    core_ref, weighted_ref, near_ref, far_ref, squared_ref, mask_ref,
    send_ref, keep_ref, evidence_ref,
    score_ref, spread_ref, columns_ref, penalty_ref,
):
    rows_per, num_rows, width = weighted_ref.shape
    num_images, orients = mask_ref.shape
    half = rows_per // 2
    tile_len = width // 2
    trials = num_rows // num_images
    near_base = core_ref[0] * half
    far_base = (1 - core_ref[0]) * half
    halves = ((near_base, near_ref), (far_base, far_ref))
    penalty = jnp.zeros((num_images, orients), f32)
    for base, slices_ref in halves:
        for p in range(half):
            piece = slices_ref[p * orients : (p + 1) * orients, :].astype(f32)
            power = piece[:, :tile_len] ** 2 + piece[:, tile_len:] ** 2
            penalty += lax.dot_general(
                0.5 * squared_ref[base + p], power, (((1,), (1,)), ((), ())),
                precision=precise, preferred_element_type=f32,
            )
    penalty_ref[...] = penalty
    chunk = 256
    for start in range(0, num_rows, chunk):
        total = jnp.zeros((chunk, orients), f32)
        for base, slices_ref in halves:
            for p in range(half):
                total += lax.dot_general(
                    weighted_ref[base + p, start : start + chunk, :],
                    slices_ref[p * orients : (p + 1) * orients, :],
                    (((1,), (1,)), ((), ())), preferred_element_type=f32,
                )
        for index in range(start // trials, (start + chunk) // trials):
            low = index * trials - start
            row = total[low : low + trials, :] - penalty_ref[index : index + 1, :]
            row = jnp.where(mask_ref[index : index + 1, :] > 0.0, row, LOWEST)
            score_ref[index * trials : (index + 1) * trials, :] = row
            columns_ref[index : index + 1, :] = jnp.max(row, axis=0, keepdims=True)
    highest = jnp.max(columns_ref[...], axis=1, keepdims=True)
    for index in range(num_images):
        rows = slice(index * trials, (index + 1) * trials)
        expo = jnp.exp(score_ref[rows, :] - highest[index : index + 1, :])
        score_ref[rows, :] = expo
        columns_ref[index : index + 1, :] = jnp.sum(expo, axis=0, keepdims=True)
    sums = jnp.sum(columns_ref[...], axis=1, keepdims=True)
    evidence_ref[...] = jnp.broadcast_to(highest + jnp.log(sums), evidence_ref.shape)
    inverse = 1.0 / sums
    columns_ref[...] = columns_ref[...] * inverse
    for index in range(num_images):
        rows = slice(index * trials, (index + 1) * trials)
        spread_ref[rows, :] = (score_ref[rows, :] * inverse[index : index + 1, :]).astype(bf16)
    spread = spread_ref[...]
    for base, back_ref in ((far_base, send_ref), (near_base, keep_ref)):
        for p in range(half):
            rows = slice(p * orients, (p + 1) * orients)
            back_ref[rows, :width] = lax.dot_general(
                spread, weighted_ref[base + p], (((0,), (0,)), ((), ())),
                preferred_element_type=f32,
            ).astype(back_ref.dtype)
            back_ref[rows, width:] = lax.dot_general(
                columns_ref[...], squared_ref[base + p], (((0,), (0,)), ((), ())),
                precision=precise, preferred_element_type=f32,
            ).astype(back_ref.dtype)


def split(value):
    high = value.astype(bf16)
    return high, (value - high.astype(f32)).astype(bf16)


def dot_split(value, high_ref, low_ref):
    rows = value.shape[0]
    high, low = split(value)
    both = jnp.concatenate([high, low], axis=0)
    by_high = jnp.dot(both, high_ref[...], preferred_element_type=f32)
    by_low = jnp.dot(high, low_ref[...], preferred_element_type=f32)
    return by_high[:rows] + (by_high[rows:] + by_low)


def tables_kernel(cos_high_ref, cos_low_ref, sin_high_ref, sin_low_ref):
    length = cos_high_ref.shape[0]
    chunk = min(length, 64)

    def one_chunk(index, carry):
        base = pl.multiple_of(index * chunk, chunk)
        row = lax.broadcasted_iota(jnp.int32, (chunk, length), 0) + base
        column = lax.broadcasted_iota(jnp.int32, (chunk, length), 1)
        turns = (row * column % length).astype(f32) * (-1.0 / length)
        cosine, sine = cos_sin_turns(turns)
        rows = pl.ds(base, chunk)
        norming = 1.0 / math.sqrt(length)
        high, low = split(cosine * norming)
        cos_high_ref[rows, :] = high
        cos_low_ref[rows, :] = low
        high, low = split(sine * norming)
        sin_high_ref[rows, :] = high
        sin_low_ref[rows, :] = low
        return carry

    lax.fori_loop(0, length // chunk, one_chunk, 0)


def lines_kernel(
    mix_near_ref, mix_far_ref, near_ref, far_ref,
    cos_high_ref, cos_low_ref, sin_high_ref, sin_low_ref, out_ref,
):
    tiles = mix_near_ref.shape[0]
    full = near_ref.shape[1]
    tile_len = full // 3
    members, depth, packed = out_ref.shape
    per_line = tiles // depth
    total = jnp.zeros((2 * tiles, full), f32)
    for mix_ref, rows_ref in ((mix_near_ref, near_ref), (mix_far_ref, far_ref)):
        both = jnp.concatenate(split(mix_ref[...]), axis=0)
        total += jnp.dot(both, rows_ref[...], preferred_element_type=f32)
    acc = total[:tiles] + total[tiles:]
    real, imag = [], []
    for q in range(per_line):
        rows = slice(q * depth, (q + 1) * depth)
        denominator = acc[rows, 2 * tile_len :] + 1.0
        real.append(acc[rows, :tile_len] / denominator)
        imag.append(acc[rows, tile_len : 2 * tile_len] / denominator)
    field = jnp.concatenate(
        [jnp.concatenate(real, axis=1), jnp.concatenate(imag, axis=1)], axis=0
    )
    by_cos = dot_split(field, cos_high_ref, cos_low_ref)
    by_sin = dot_split(field, sin_high_ref, sin_low_ref)
    lines_re = by_cos[:depth] - by_sin[depth:]
    lines_im = by_sin[:depth] + by_cos[depth:]
    block = packed // 2
    for member in range(members):
        columns = slice(member * block, (member + 1) * block)
        out_ref[member, :, :block] = lines_re[:, columns]
        out_ref[member, :, block:] = lines_im[:, columns]


def depth_kernel(
    columns_ref, correction_ref, cos_high_ref, cos_low_ref, sin_high_ref, sin_low_ref, out_ref
):
    block = out_ref.shape[1]
    field = jnp.transpose(columns_ref[...])
    by_cos = dot_split(field, cos_high_ref, cos_low_ref)
    by_sin = dot_split(field, sin_high_ref, sin_low_ref)
    correction = correction_ref[...]
    out_ref[0] = (by_cos[:block] - by_sin[block:]) / correction
    out_ref[1] = (by_sin[:block] + by_cos[block:]) / correction


VMEM = pltpu.VMEM


def weigh(images, ctf, noise_weight, shifts):
    num_images, rows_per, width = images.shape
    trials = shifts.shape[2]
    columns = jnp.transpose(shifts, (0, 2, 1)).reshape(num_images * trials, 2)
    return pl.pallas_call(
        weighted_kernel,
        out_shape=jax.ShapeDtypeStruct((rows_per, num_images * trials, width), bf16),
        in_specs=[pl.BlockSpec(memory_space=VMEM)] * 4,
        out_specs=pl.BlockSpec(memory_space=VMEM),
        compiler_params=pltpu.CompilerParams(vmem_limit_bytes=24 << 20),
        name="weigh",
    )(images, ctf, noise_weight, columns)


def expect(core, weighted, near, far, squared, mask):
    rows_per, num_rows, width = weighted.shape
    num_images, orients = mask.shape
    half = jax.ShapeDtypeStruct((near.shape[0], width + width // 2), bf16)
    return pl.pallas_call(
        expectation_kernel,
        out_shape=(half, half, jax.ShapeDtypeStruct((num_images, 128), f32)),
        in_specs=[pl.BlockSpec(memory_space=pltpu.SMEM)] + [pl.BlockSpec(memory_space=VMEM)] * 5,
        out_specs=(pl.BlockSpec(memory_space=VMEM),) * 3,
        scratch_shapes=[
            VMEM((num_rows, orients), f32),
            VMEM((num_rows, orients), bf16),
            VMEM((num_images, orients), f32),
            VMEM((num_images, orients), f32),
        ],
        compiler_params=pltpu.CompilerParams(vmem_limit_bytes=24 << 20),
        name="expect",
    )(core, weighted, near, far, squared, mask)


def dft_tables(length):
    return pl.pallas_call(
        tables_kernel,
        out_shape=(jax.ShapeDtypeStruct((length, length), bf16),) * 4,
        out_specs=(pl.BlockSpec(memory_space=VMEM),) * 4,
        compiler_params=pltpu.CompilerParams(vmem_limit_bytes=8 << 20),
        name="tables",
    )()


def in_vmem(kernel, name, shape, *operands):
    return pl.pallas_call(
        kernel,
        out_shape=jax.ShapeDtypeStruct(shape, f32),
        in_specs=[pl.BlockSpec(memory_space=VMEM)] * len(operands),
        out_specs=pl.BlockSpec(memory_space=VMEM),
        compiler_params=pltpu.CompilerParams(vmem_limit_bytes=16 << 20),
        name=name,
    )(*operands)


def centred_sinc(positions, length):
    centred = ((positions + length // 2) % length - length // 2).astype(f32) / length
    return jnp.sinc(centred) ** 2


def exchange(pieces, axis):
    return lax.all_to_all(pieces, axis, split_axis=0, concat_axis=0, tiled=True)


def scatter_sum(pieces, axis):
    return jnp.sum(exchange(pieces, axis).astype(f32), axis=0)


def gather_all(piece, axis, count):
    return exchange(jnp.broadcast_to(piece[None], (count,) + piece.shape), axis)


def swap(value):
    return lax.ppermute(value, "core", [(0, 1), (1, 0)])


def on_device(volume, images, ctf, noise_weight, shifts, orient, counts, tile_map, interp):
    n_vol = lax.axis_size("vol")
    n_chip = lax.axis_size("chip")
    n_img = n_chip * 2
    vol_index = lax.axis_index("vol")
    core = lax.axis_index("core")
    img_index = lax.axis_index("chip") * 2 + core
    slab_depth, planes_dev, per_line, width = volume.shape
    tile_len = width // 2
    planes_all = planes_dev * n_img
    depth_len = slab_depth * n_vol
    line_len = per_line * tile_len
    orients, rows_per, terms = tile_map.shape
    half = orients * rows_per // 2
    slots = orient.shape[1]
    tiles = slab_depth * per_line
    block = half // n_chip
    part = block // n_vol
    full = width + tile_len

    tile_of = jnp.transpose(tile_map, (2, 1, 0)).reshape(terms, 2 * half)
    factor_of = jnp.transpose(interp, (2, 1, 0)).reshape(terms, 2 * half)
    tile_depth = tile_of // (planes_all * per_line)
    tile_plane = tile_of // per_line % planes_all
    tile_quarter = tile_of % per_line
    owned = (tile_depth // slab_depth == vol_index) & (tile_plane == img_index)
    local = jnp.where(owned, tile_quarter * slab_depth + tile_depth - vol_index * slab_depth, -1)

    def mixing_of(which):
        mine = lax.dynamic_slice_in_dim(local, which * half, half, axis=1)
        factor = lax.dynamic_slice_in_dim(factor_of, which * half, half, axis=1)
        hit = mine[:, None, :] == jnp.arange(tiles, dtype=jnp.int32)[None, :, None]
        return jnp.sum(jnp.where(hit, factor[:, None, :], 0.0), axis=0)

    mix_near = mixing_of(core)
    mix_far = mixing_of(1 - core)
    flat_tiles = jnp.transpose(volume, (2, 1, 0, 3)).reshape(tiles, width)
    mix_dot = functools.partial(
        lax.dot_general, dimension_numbers=(((0,), (0,)), ((), ())), precision=precise
    )
    mine = mix_dot(mix_near, flat_tiles) + swap(mix_dot(mix_far, flat_tiles))
    mine = scatter_sum(mine.reshape(n_chip, block, width), "chip")
    mine = scatter_sum(mine.reshape(n_vol, part, width), "vol").astype(bf16)
    mine = gather_all(mine, "vol", n_vol).reshape(block, width)
    near = gather_all(mine, "chip", n_chip).reshape(half, width)
    far = swap(near)

    weighted = weigh(images, ctf, noise_weight, shifts)
    squared = jnp.transpose(noise_weight * ctf * ctf, (1, 0, 2))
    usable = jnp.arange(slots, dtype=jnp.int32)[None, :] < counts[:, None]
    listed = jnp.where(usable, orient, -1)
    mask = jnp.max(
        (listed[:, :, None] == jnp.arange(orients, dtype=jnp.int32)).astype(f32), axis=1
    )
    tables_line = dft_tables(line_len)
    tables_depth = tables_line if depth_len == line_len else dft_tables(depth_len)
    send, keep, evidence = expect(
        core.astype(jnp.int32).reshape(1), weighted, near, far, squared, mask
    )

    rows = (keep.astype(f32) + swap(send).astype(f32)).astype(bf16)
    rows = scatter_sum(rows.reshape(n_chip, block, full), "chip")
    rows = scatter_sum(rows.reshape(n_vol, part, full), "vol").astype(bf16)
    rows = gather_all(rows, "vol", n_vol).reshape(block, full)
    rows_near = gather_all(rows, "chip", n_chip).reshape(half, full)
    rows_far = swap(rows_near)
    y_block = line_len // n_vol
    lines = in_vmem(
        lines_kernel, "lines", (n_vol, slab_depth, 2 * y_block),
        mix_near, mix_far, rows_near, rows_far, *tables_line,
    )
    columns = exchange(lines, "vol").reshape(depth_len, 2 * y_block)
    depth_corr = centred_sinc(jnp.arange(depth_len, dtype=jnp.int32), depth_len)
    line_corr = centred_sinc(vol_index * y_block + jnp.arange(y_block, dtype=jnp.int32), line_len)
    correction = line_corr[:, None] * depth_corr[None, :]
    real_space = in_vmem(
        depth_kernel, "depth", (2, y_block, depth_len), columns, correction, *tables_depth
    )
    return (jnp.transpose(real_space, (0, 2, 1))[:, :, None, :], evidence[:, 0])


def solution(mesh):
    devices = mesh.devices
    n_img, n_vol = devices.shape
    finer = jax.sharding.Mesh(devices.reshape(n_img // 2, 2, n_vol), ("chip", "core", "vol"))
    images = ("chip", "core", "vol")
    placed = (
        P("vol", ("chip", "core"), None, None),
        P(images, None, None),
        P(images, None, None),
        P(images, None, None),
        P(images, None, None),
        P(images, None),
        P(images),
        P(),
        P(),
    )
    return jax.shard_map(
        on_device,
        mesh=finer,
        in_specs=placed,
        out_specs=(P(None, None, ("chip", "core"), "vol"), P(images)),
        check_vma=False,
    )
```

profile of v0, /device:TPU:1, one launch (start us, length us, event | category | flops | bytes accessed | tf_op | source)
XLA Modules:
  0.0 183.1 jit_solution(9538148762754005199)
XLA Ops:
  0.6 0.9 copy.24
  1.5 0.1 reshape.159
  1.6 0.9 copy.25
  2.5 0.1 reshape.160
  2.5 0.1 fusion.9
  2.7 0.9 copy.27
  3.6 0.2 select_reduce_fusion.mix_far_ref
  3.7 0.8 fusion.39
  4.6 8.7 %collective-permute-start = (f32[768,256]{1,0:T(8,128)S(1)}, f32[768,256]{1,0:T(8,128)S(1)}, u32[]{:S(2)}, u32[]{:S(2)}) collective-permute-start(f32[768,256]{1,0:T(8,128)S(1)} %fusion.39), channel_id=1, source_target_pairs={{0,32},{32,0},{1,33},{33,1},{2,34},{34,2},{3,35},{35,3},{4,36},{36... | collective-permute-start | bytes 2359304 | tf_op jit(solution)/shard_map/ppermute | solution.py:287
  13.3 0.2 select_reduce_fusion.1.mix_near_ref
  13.5 1.7 collective-permute-done
  15.2 0.8 convolution_add_fusion
  16.0 15.0 %all_to_all.45 = f32[8,96,256]{2,1,0:T(8,128)S(1)} all-to-all(f32[8,96,256]{2,1,0:T(8,128)S(1)} %bitcast.30), channel_id=1, replica_groups=mesh['chip'=8,'core'=2,'vol'=32] {'chip'}, dimensions={0} | all-to-all | bytes 1572864 | tf_op jit(solution)/shard_map/all_to_all | solution.py:275
  31.1 0.0 copy-start.4
  31.1 0.0 copy-start.5
  31.1 0.0 copy-start.3
  31.1 0.1 reduce_sum.56
  31.1 0.0 copy-start
  31.2 0.0 copy-start.1
  31.2 0.0 copy-start.2
  31.2 22.5 %all_to_all.46 = f32[32,3,256]{2,1,0:T(4,128)S(1)} all-to-all(f32[32,3,256]{2,1,0:T(4,128)S(1)} %reshape.165), channel_id=1, replica_groups=mesh['chip'=8,'core'=2,'vol'=32] {'vol'}, dimensions={0} | all-to-all | bytes 196608 | tf_op jit(solution)/shard_map/all_to_all | solution.py:275
  53.8 14.3 %all_to_all.47 = bf16[32,3,256]{2,1,0:T(4,128)(2,1)S(1)} all-to-all(bf16[32,3,256]{2,1,0:T(4,128)(2,1)S(1)} %broadcast_in_dim.78), channel_id=1, replica_groups=mesh['chip'=8,'core'=2,'vol'=32] {'vol'}, dimensions={0} | all-to-all | bytes 98304 | tf_op jit(solution)/shard_map/all_to_all | solution.py:275
  68.2 9.9 %all_to_all.48 = bf16[8,96,256]{2,1,0:T(8,128)(2,1)S(1)} all-to-all(bf16[8,96,256]{2,1,0:T(8,128)(2,1)S(1)} %broadcast_in_dim.80), channel_id=1, replica_groups=mesh['chip'=8,'core'=2,'vol'=32] {'chip'}, dimensions={0} | all-to-all | bytes 786432 | tf_op jit(solution)/shard_map/all_to_all | solution.py:275
  78.1 7.0 %collective-permute-start.1 = (bf16[768,256]{1,0:T(8,128)(2,1)S(1)}, bf16[768,256]{1,0:T(8,128)(2,1)S(1)}, u32[]{:S(2)}, u32[]{:S(2)}) collective-permute-start(bf16[768,256]{1,0:T(8,128)(2,1)S(1)} %bitcast.27), channel_id=1, source_target_pairs={{0,32},{32,0},{1,33},{33,1},{2,34},{34,2},{3,35},{35,3},{4,36},{36... | collective-permute-start | bytes 1179656 | tf_op jit(solution)/shard_map/ppermute | solution.py:287
  85.1 0.0 copy-done.4
  85.1 0.0 copy-done.5
  85.1 0.1 fusion.14
  85.2 0.0 copy-done.3
  85.2 0.3 copy.26
  85.4 0.0 copy-done
  85.5 0.0 copy-done.1
  85.5 0.0 copy-done.2
  85.5 5.6 %weigh.1.weighted_ref = bf16[8,1024,256]{2,1,0:T(8,128)(2,1)S(1)} custom-call(bf16[32,8,256]{2,1,0:T(8,128)(2,1)S(1)} %copy-done.2, f32[32,8,128]{2,1,0:T(8,128)S(1)} %copy-done, f32[32,8,128]{2,1,0:T(8,128)S(1)} %copy-done.1, f32[1024,2]{1,0:T(8,128)S(1)} %bitcast.26), custom_call_target="tpu_custom_call" | custom-call | tf_op jit(solution)/shard_map/weigh/pallas_call | solution.py:218
  91.1 0.6 convert_reduce_fusion.mask_ref
  91.8 0.0 collective-permute-done.1.far_ref
  91.8 5.1 %expect.1 = (bf16[768,384]{1,0:T(8,128)(2,1)S(1)}, bf16[768,384]{1,0:T(8,128)(2,1)S(1)}, f32[32,128]{1,0:T(8,128)S(1)}) custom-call(s32[1]{0:T(128)} %bitcast.2.core_ref, bf16[8,1024,256]{2,1,0:T(8,128)(2,1)S(1)} %weigh.1.weighted_ref, bf16[768,256]{1,0:T(8,128)(2,1)S(1)} %bitcast.28, bf16[768,256]{1,0:T(8,128)(2,1)S(1)} %collective-permute-done.1.far_ref, ...), custom_call_target="tpu_custom_call" | custom-call | tf_op jit(solution)/shard_map/expect/pallas_call | solution.py:232
  96.9 1.9 %collective-permute-start.2 = (bf16[768,384]{1,0:T(8,128)(2,1)S(1)}, bf16[768,384]{1,0:T(8,128)(2,1)S(1)}, u32[]{:S(2)}, u32[]{:S(2)}) collective-permute-start(bf16[768,384]{1,0:T(8,128)(2,1)S(1)} %get-tuple-element.10), channel_id=1, source_target_pairs={{0,32},{32,0},{1,33},{33,1},{2,34},{34,2},{3,35},{35,3},{4,36},{36... | collective-permute-start | bytes 1769480 | tf_op jit(solution)/shard_map/ppermute | solution.py:287
  98.8 2.0 %collective-permute-done.2 = bf16[768,384]{1,0:T(8,128)(2,1)S(1)} collective-permute-done((bf16[768,384]{1,0:T(8,128)(2,1)S(1)}, bf16[768,384]{1,0:T(8,128)(2,1)S(1)}, u32[]{:S(2)}, u32[]{:S(2)}) %collective-permute-start.2) | collective-permute-done | bytes 589856 | tf_op jit(solution)/shard_map/ppermute | solution.py:287
  100.8 0.2 add_convert_fusion
  100.9 13.1 %all_to_all.49 = bf16[8,96,384]{2,1,0:T(8,128)(2,1)S(1)} all-to-all(bf16[8,96,384]{2,1,0:T(8,128)(2,1)S(1)} %bitcast.31), channel_id=1, replica_groups=mesh['chip'=8,'core'=2,'vol'=32] {'chip'}, dimensions={0} | all-to-all | bytes 1179648 | tf_op jit(solution)/shard_map/all_to_all | solution.py:275
  114.0 0.1 convert_reduce_fusion.1
  114.1 0.1 reshape.168
  114.2 14.5 %all_to_all.50 = f32[32,3,384]{2,1,0:T(4,128)S(1)} all-to-all(f32[32,3,384]{2,1,0:T(4,128)S(1)} %reshape.168), channel_id=1, replica_groups=mesh['chip'=8,'core'=2,'vol'=32] {'vol'}, dimensions={0} | all-to-all | bytes 294912 | tf_op jit(solution)/shard_map/all_to_all | solution.py:275
  128.7 0.1 reduce_sum.59
  128.8 16.6 %all_to_all.51 = bf16[32,3,384]{2,1,0:T(4,128)(2,1)S(1)} all-to-all(bf16[32,3,384]{2,1,0:T(4,128)(2,1)S(1)} %broadcast_in_dim.82), channel_id=1, replica_groups=mesh['chip'=8,'core'=2,'vol'=32] {'vol'}, dimensions={0} | all-to-all | bytes 147456 | tf_op jit(solution)/shard_map/all_to_all | solution.py:275
  145.4 0.1 broadcast_in_dim.83
  145.5 0.1 broadcast_in_dim.84
  145.5 10.8 %all_to_all.52 = bf16[8,96,384]{2,1,0:T(8,128)(2,1)S(1)} all-to-all(bf16[8,96,384]{2,1,0:T(8,128)(2,1)S(1)} %broadcast_in_dim.84), channel_id=1, replica_groups=mesh['chip'=8,'core'=2,'vol'=32] {'chip'}, dimensions={0} | all-to-all | bytes 1179648 | tf_op jit(solution)/shard_map/all_to_all | solution.py:275
  156.3 5.3 %collective-permute-start.3 = (bf16[768,384]{1,0:T(8,128)(2,1)S(1)}, bf16[768,384]{1,0:T(8,128)(2,1)S(1)}, u32[]{:S(2)}, u32[]{:S(2)}) collective-permute-start(bf16[768,384]{1,0:T(8,128)(2,1)S(1)} %bitcast.24), channel_id=1, source_target_pairs={{0,32},{32,0},{1,33},{33,1},{2,34},{34,2},{3,35},{35,3},{4,36},{36... | collective-permute-start | bytes 1769480 | tf_op jit(solution)/shard_map/ppermute | solution.py:287
  161.7 2.1 %tables.1 = (bf16[512,512]{1,0:T(8,128)(2,1)S(1)}, bf16[512,512]{1,0:T(8,128)(2,1)S(1)}, bf16[512,512]{1,0:T(8,128)(2,1)S(1)}, bf16[512,512]{1,0:T(8,128)(2,1)S(1)}) custom-call(), custom_call_target="tpu_custom_call" | custom-call | tf_op jit(solution)/shard_map/tables/pallas_call | solution.py:249
  163.8 0.0 collective-permute-done.3.far_ref
  163.8 1.0 lines.1
  164.8 0.8 reshape.172
  165.6 3.9 %all-to-all-start.8 = ((f32[32,1,512]{2,1,0:T(1,128)}), f32[32,1,512]{2,1,0:T(1,128)S(1)}, u32[]{:S(2)}, u32[]{:S(2)}) async-start(f32[32,1,512]{2,1,0:T(1,128)} %reshape.172), calls=%async_computation.8 | async-start | bytes 131072 | tf_op jit(solution)/shard_map/all_to_all | solution.py:275
  169.5 0.1 broadcast_multiply_fusion.correction_ref
  169.5 0.6 slice_reduce_fusion
  170.2 10.4 %all-to-all-done.8 = f32[32,1,512]{2,1,0:T(1,128)S(1)} async-done(((f32[32,1,512]{2,1,0:T(1,128)}), f32[32,1,512]{2,1,0:T(1,128)S(1)}, u32[]{:S(2)}, u32[]{:S(2)}) %all-to-all-start.8) | async-done | bytes 65568 | tf_op jit(solution)/shard_map/all_to_all | solution.py:275
  180.6 0.5 broadcast.284
  181.1 0.8 reduce.2
  181.9 0.1 reshape.173
  182.0 1.1 depth.1
  (11 shorter events, 0.4 us)
Async XLA Ops:
  4.6 10.6 %collective-permute-start = (f32[768,256]{1,0:T(8,128)S(1)}, f32[768,256]{1,0:T(8,128)S(1)}, u32[]{:S(2)}, u32[]{:S(2)}) collective-permute-start(f32[768,256]{1,0:T(8,128)S(1)} %fusion.39), channel_id=1, source_target_pairs={{0,32},{32,0},{1,33},{33,1},{2,34},{34,2},{3,35},{35,3},{4,36},{36... | collective-permute-start | bytes 2359304 | tf_op jit(solution)/shard_map/ppermute | solution.py:287
  31.1 54.0 %copy-start.4 = (s32[32,64]{1,0:T(8,128)S(1)}, s32[32,64]{1,0:T(8,128)}, u32[]{:S(2)}) copy-start(s32[32,64]{1,0:T(8,128)} %param.14) | copy-start | bytes 24580
  31.1 54.0 %copy-start.5 = (s32[32]{0:T(128)S(1)}, s32[32]{0:T(128)}, u32[]{:S(2)}) copy-start(s32[32]{0:T(128)} %param.15) | copy-start | bytes 388
  31.1 54.1 %copy-start.3 = (f32[32,2,32]{2,1,0:T(2,128)S(1)}, f32[32,2,32]{2,1,0:T(2,128)}, u32[]{:S(2)}) copy-start(f32[32,2,32]{2,1,0:T(2,128)} %param.13) | copy-start | bytes 24580
  31.1 54.3 %copy-start = (f32[32,8,128]{2,1,0:T(8,128)S(1)}, f32[32,8,128]{2,1,0:T(8,128)}, u32[]{:S(2)}) copy-start(f32[32,8,128]{2,1,0:T(8,128)} %ctf_ref.1) | copy-start | bytes 393220
  31.2 54.3 %copy-start.1 = (f32[32,8,128]{2,1,0:T(8,128)S(1)}, f32[32,8,128]{2,1,0:T(8,128)}, u32[]{:S(2)}) copy-start(f32[32,8,128]{2,1,0:T(8,128)} %noise_ref.1) | copy-start | bytes 393220
  31.2 54.3 %copy-start.2 = (bf16[32,8,256]{2,1,0:T(8,128)(2,1)S(1)}, bf16[32,8,256]{2,1,0:T(8,128)(2,1)}, u32[]{:S(2)}) copy-start(bf16[32,8,256]{2,1,0:T(8,128)(2,1)} %images_ref.1) | copy-start | bytes 393220
  78.1 13.7 %collective-permute-start.1 = (bf16[768,256]{1,0:T(8,128)(2,1)S(1)}, bf16[768,256]{1,0:T(8,128)(2,1)S(1)}, u32[]{:S(2)}, u32[]{:S(2)}) collective-permute-start(bf16[768,256]{1,0:T(8,128)(2,1)S(1)} %bitcast.27), channel_id=1, source_target_pairs={{0,32},{32,0},{1,33},{33,1},{2,34},{34,2},{3,35},{35,3},{4,36},{36... | collective-permute-start | bytes 1179656 | tf_op jit(solution)/shard_map/ppermute | solution.py:287
  96.9 3.9 %collective-permute-start.2 = (bf16[768,384]{1,0:T(8,128)(2,1)S(1)}, bf16[768,384]{1,0:T(8,128)(2,1)S(1)}, u32[]{:S(2)}, u32[]{:S(2)}) collective-permute-start(bf16[768,384]{1,0:T(8,128)(2,1)S(1)} %get-tuple-element.10), channel_id=1, source_target_pairs={{0,32},{32,0},{1,33},{33,1},{2,34},{34,2},{3,35},{35,3},{4,36},{36... | collective-permute-start | bytes 1769480 | tf_op jit(solution)/shard_map/ppermute | solution.py:287
  156.3 7.5 %collective-permute-start.3 = (bf16[768,384]{1,0:T(8,128)(2,1)S(1)}, bf16[768,384]{1,0:T(8,128)(2,1)S(1)}, u32[]{:S(2)}, u32[]{:S(2)}) collective-permute-start(bf16[768,384]{1,0:T(8,128)(2,1)S(1)} %bitcast.24), channel_id=1, source_target_pairs={{0,32},{32,0},{1,33},{33,1},{2,34},{34,2},{3,35},{35,3},{4,36},{36... | collective-permute-start | bytes 1769480 | tf_op jit(solution)/shard_map/ppermute | solution.py:287
  165.6 15.0 %all-to-all-start.8 = ((f32[32,1,512]{2,1,0:T(1,128)}), f32[32,1,512]{2,1,0:T(1,128)S(1)}, u32[]{:S(2)}, u32[]{:S(2)}) async-start(f32[32,1,512]{2,1,0:T(1,128)} %reshape.172), calls=%async_computation.8 | async-start | bytes 131072 | tf_op jit(solution)/shard_map/all_to_all | solution.py:275
where the time goes:
time: 184 us; the launch traced here: 183 us
  blocking collectives  117 us (64%)
  starting transfers between devices  26.8 us (15%)
  Pallas kernels  14.9 us (8%)
  waiting for transfers between devices  14.1 us (8%)
  local copies, waits for them, and re-layouts  5.47 us (3%)
  other arithmetic  2.53 us (1%)
    all_to_all x8, blocking collectives, exchange(): return lax.all_to_all(pieces, axis, split_axis=0, concat_axis=0, tiled=True)  117 us
    ppermute x4, starting transfers between devices, swap(): return lax.ppermute(value, 'core', [(0, 1), (1, 0)])  23 us
    all_to_all x1, waiting for transfers between devices, exchange(): return lax.all_to_all(pieces, axis, split_axis=0, concat_axis=0, tiled=True)  10.4 us
    pallas_call x1, Pallas kernels, weigh(): pl.pallas_call(weighted_kernel, out_shape=jax.ShapeDtypeStruct((rows_per,...  5.61 us
    pallas_call x1, Pallas kernels, expect(): pl.pallas_call(expectation_kernel, out_shape=(half, half, jax.ShapeDtypeS...  5.08 us
    all_to_all x1, starting transfers between devices, exchange(): return lax.all_to_all(pieces, axis, split_axis=0, concat_axis=0, tiled=True)  3.85 us
    ppermute x4, waiting for transfers between devices, swap(): return lax.ppermute(value, 'core', [(0, 1), (1, 0)])  3.69 us
  transfers between devices with their start and end apart: 5, of which 3 were waited for; matrix products, arithmetic and copies ran while one was open for 1% of the time, Pallas kernels for 4%

commit v1 on v0

--- a/solution.py
+++ b/solution.py
@@ -139,7 +139,7 @@
     return by_high[:rows] + (by_high[rows:] + by_low)
 
 
-def tables_kernel(cos_high_ref, cos_low_ref, sin_high_ref, sin_low_ref):
+def tables_kernel(order_ref, cos_high_ref, cos_low_ref, sin_high_ref, sin_low_ref):
     length = cos_high_ref.shape[0]
     chunk = min(length, 64)
 
@@ -162,45 +162,90 @@
     lax.fori_loop(0, length // chunk, one_chunk, 0)
 
 
-def lines_kernel(
-    mix_near_ref, mix_far_ref, near_ref, far_ref,
-    cos_high_ref, cos_low_ref, sin_high_ref, sin_low_ref, out_ref,
+def placing_kernel(index_ref, factor_ref, out_ref):
+    terms = index_ref.shape[0]
+    halves, tiles, half = out_ref.shape
+    lanes, chunk = 128, 64
+    for which in range(halves):
+        for low in range(0, half, lanes):
+            columns = slice(which * half + low, which * half + low + lanes)
+            index = index_ref[:, columns]
+            factor = factor_ref[:, columns]
+            merged = jnp.zeros_like(factor)
+            for k in range(terms):
+                merged += jnp.where(index == index[k : k + 1, :], factor[k : k + 1, :], 0.0)
+            index_of = [jnp.broadcast_to(index[k : k + 1, :], (8, lanes)) for k in range(terms)]
+            value_of = [jnp.broadcast_to(merged[k : k + 1, :], (8, lanes)) for k in range(terms)]
+
+            def one_chunk(step, carry):
+                base = pl.multiple_of(step * chunk, chunk)
+                row = lax.broadcasted_iota(jnp.int32, (8, lanes), 0) + base
+                pieces = []
+                for shift in range(0, chunk, 8):
+                    value = jnp.zeros((8, lanes), f32)
+                    for k in range(terms):
+                        value = jnp.where(row + shift == index_of[k], value_of[k], value)
+                    pieces.append(value)
+                out_ref[which, pl.ds(base, chunk), low : low + lanes] = jnp.concatenate(
+                    pieces, axis=0
+                ).astype(bf16)
+                return carry
+
+            lax.fori_loop(0, tiles // chunk, one_chunk, 0)
+
+
+def gather_kernel(place_scalar_ref, place_ref, rows_ref, acc_ref):
+    tiles = acc_ref.shape[0]
+    chunk = min(tiles, 256)
+    core = place_scalar_ref[0]
+    for low in range(0, tiles, chunk):
+        acc_ref[low : low + chunk, :] = jnp.dot(
+            place_ref[core, low : low + chunk, :], rows_ref[...], preferred_element_type=f32
+        )
+
+
+def finish_kernel(
+    place_scalar_ref, place_ref, acc_ref, rows_ref, correction_ref,
+    line_cos_high_ref, line_cos_low_ref, line_sin_high_ref, line_sin_low_ref,
+    cos_high_ref, cos_low_ref, sin_high_ref, sin_low_ref, out_ref, field_ref,
 ):
-    tiles = mix_near_ref.shape[0]
-    full = near_ref.shape[1]
+    block, depth = correction_ref.shape
+    tiles, full = acc_ref.shape
     tile_len = full // 3
-    members, depth, packed = out_ref.shape
-    per_line = tiles // depth
-    total = jnp.zeros((2 * tiles, full), f32)
-    for mix_ref, rows_ref in ((mix_near_ref, near_ref), (mix_far_ref, far_ref)):
-        both = jnp.concatenate(split(mix_ref[...]), axis=0)
-        total += jnp.dot(both, rows_ref[...], preferred_element_type=f32)
-    acc = total[:tiles] + total[tiles:]
-    real, imag = [], []
-    for q in range(per_line):
-        rows = slice(q * depth, (q + 1) * depth)
-        denominator = acc[rows, 2 * tile_len :] + 1.0
-        real.append(acc[rows, :tile_len] / denominator)
-        imag.append(acc[rows, tile_len : 2 * tile_len] / denominator)
-    field = jnp.concatenate(
-        [jnp.concatenate(real, axis=1), jnp.concatenate(imag, axis=1)], axis=0
-    )
-    by_cos = dot_split(field, cos_high_ref, cos_low_ref)
-    by_sin = dot_split(field, sin_high_ref, sin_low_ref)
-    lines_re = by_cos[:depth] - by_sin[depth:]
-    lines_im = by_sin[:depth] + by_cos[depth:]
-    block = packed // 2
-    for member in range(members):
-        columns = slice(member * block, (member + 1) * block)
-        out_ref[member, :, :block] = lines_re[:, columns]
-        out_ref[member, :, block:] = lines_im[:, columns]
-
-
-def depth_kernel(
-    columns_ref, correction_ref, cos_high_ref, cos_low_ref, sin_high_ref, sin_low_ref, out_ref
-):
-    block = out_ref.shape[1]
-    field = jnp.transpose(columns_ref[...])
+    other = 1 - place_scalar_ref[0]
+    first = pl.multiple_of(place_scalar_ref[1] * block, block)
+    chosen = pl.ds(first, block)
+    chunk = min(depth, 256)
+    across = (((1,), (1,)), ((), ()))
+    for z in range(0, depth, chunk):
+        total_re = jnp.zeros((block, chunk), f32)
+        total_im = jnp.zeros((block, chunk), f32)
+        for q in range(tiles // depth):
+            low = q * depth + z
+            tile = acc_ref[low : low + chunk, :] + jnp.dot(
+                place_ref[other, low : low + chunk, :], rows_ref[...], preferred_element_type=f32
+            )
+            columns = slice(q * tile_len, (q + 1) * tile_len)
+            high_table = jnp.concatenate(
+                [line_cos_high_ref[chosen, columns], line_sin_high_ref[chosen, columns]], axis=0
+            )
+            low_table = jnp.concatenate(
+                [line_cos_low_ref[chosen, columns], line_sin_low_ref[chosen, columns]], axis=0
+            )
+            both_tables = jnp.concatenate([high_table, low_table], axis=0)
+            inverse = 1.0 / (tile[:, 2 * tile_len :] + 1.0)
+            parts = []
+            for low_lane in (0, tile_len):
+                high, low_part = split(tile[:, low_lane : low_lane + tile_len] * inverse)
+                by_high = lax.dot_general(both_tables, high, across, preferred_element_type=f32)
+                by_low = lax.dot_general(high_table, low_part, across, preferred_element_type=f32)
+                parts.append(by_high[: 2 * block] + (by_high[2 * block :] + by_low))
+            by_re, by_im = parts
+            total_re += by_re[:block] - by_im[block:]
+            total_im += by_re[block:] + by_im[:block]
+        field_ref[:block, z : z + chunk] = total_re
+        field_ref[block:, z : z + chunk] = total_im
+    field = field_ref[...]
     by_cos = dot_split(field, cos_high_ref, cos_low_ref)
     by_sin = dot_split(field, sin_high_ref, sin_low_ref)
     correction = correction_ref[...]
@@ -220,7 +265,11 @@
         out_shape=jax.ShapeDtypeStruct((rows_per, num_images * trials, width), bf16),
         in_specs=[pl.BlockSpec(memory_space=VMEM)] * 4,
         out_specs=pl.BlockSpec(memory_space=VMEM),
-        compiler_params=pltpu.CompilerParams(vmem_limit_bytes=24 << 20),
+        compiler_params=pltpu.CompilerParams(vmem_limit_bytes=16 << 20),
+        cost_estimate=pl.CostEstimate(
+            flops=40 * rows_per * num_images * trials * width,
+            bytes_accessed=2 * rows_per * num_images * trials * width, transcendentals=0,
+        ),
         name="weigh",
     )(images, ctf, noise_weight, columns)
 
@@ -245,25 +294,30 @@
     )(core, weighted, near, far, squared, mask)
 
 
-def dft_tables(length):
+def dft_tables(order, length):
     return pl.pallas_call(
         tables_kernel,
         out_shape=(jax.ShapeDtypeStruct((length, length), bf16),) * 4,
+        in_specs=[pl.BlockSpec(memory_space=pltpu.SMEM)],
         out_specs=(pl.BlockSpec(memory_space=VMEM),) * 4,
         compiler_params=pltpu.CompilerParams(vmem_limit_bytes=8 << 20),
+        cost_estimate=pl.CostEstimate(flops=30 * length * length, bytes_accessed=8 * length * length, transcendentals=0),
         name="tables",
-    )()
-
-
-def in_vmem(kernel, name, shape, *operands):
+    )(order)
+
+
+def in_vmem(kernel, name, out_shape, scalars, *operands, scratch=(), cost=None):
     return pl.pallas_call(
         kernel,
-        out_shape=jax.ShapeDtypeStruct(shape, f32),
-        in_specs=[pl.BlockSpec(memory_space=VMEM)] * len(operands),
+        out_shape=out_shape,
+        in_specs=[pl.BlockSpec(memory_space=pltpu.SMEM)] * len(scalars)
+        + [pl.BlockSpec(memory_space=VMEM)] * len(operands),
         out_specs=pl.BlockSpec(memory_space=VMEM),
-        compiler_params=pltpu.CompilerParams(vmem_limit_bytes=16 << 20),
+        scratch_shapes=list(scratch),
+        compiler_params=pltpu.CompilerParams(vmem_limit_bytes=24 << 20),
+        cost_estimate=cost,
         name=name,
-    )(*operands)
+    )(*scalars, *operands)
 
 
 def centred_sinc(positions, length):
@@ -329,11 +383,30 @@
     )
     mine = mix_dot(mix_near, flat_tiles) + swap(mix_dot(mix_far, flat_tiles))
     mine = scatter_sum(mine.reshape(n_chip, block, width), "chip")
-    mine = scatter_sum(mine.reshape(n_vol, part, width), "vol").astype(bf16)
-    mine = gather_all(mine, "vol", n_vol).reshape(block, width)
-    near = gather_all(mine, "chip", n_chip).reshape(half, width)
-    far = swap(near)
-
+    plane_index = jnp.where(tile_plane == img_index, tile_quarter * depth_len + tile_depth, -1)
+    scalars = jnp.stack([core, vol_index]).astype(jnp.int32)
+    pieces, plane_index, factor_in, order = lax.optimization_barrier(
+        (mine.reshape(n_vol, part, width), plane_index, factor_of, scalars)
+    )
+    place = in_vmem(
+        placing_kernel, "placing",
+        jax.ShapeDtypeStruct((2, depth_len * per_line, half), bf16), (), plane_index, factor_in,
+        cost=pl.CostEstimate(
+            flops=40 * depth_len * per_line * half, bytes_accessed=4 * depth_len * per_line * half,
+            transcendentals=0,
+        ),
+    )
+    tables_line = dft_tables(order, line_len)
+    tables_depth = tables_line if depth_len == line_len else dft_tables(order, depth_len)
+    arrived = exchange(pieces, "vol")
+    arrived, place, tables_line, tables_depth = lax.optimization_barrier(
+        (arrived, place, tables_line, tables_depth)
+    )
+    mine = jnp.sum(arrived, axis=0).astype(bf16)
+    pieces = jnp.broadcast_to(mine[None], (n_vol,) + mine.shape)
+    pieces, images, ctf, noise_weight, shifts, orient, counts = lax.optimization_barrier(
+        (pieces, images, ctf, noise_weight, shifts, orient, counts)
+    )
     weighted = weigh(images, ctf, noise_weight, shifts)
     squared = jnp.transpose(noise_weight * ctf * ctf, (1, 0, 2))
     usable = jnp.arange(slots, dtype=jnp.int32)[None, :] < counts[:, None]
@@ -341,11 +414,19 @@
     mask = jnp.max(
         (listed[:, :, None] == jnp.arange(orients, dtype=jnp.int32)).astype(f32), axis=1
     )
-    tables_line = dft_tables(line_len)
-    tables_depth = tables_line if depth_len == line_len else dft_tables(depth_len)
-    send, keep, evidence = expect(
-        core.astype(jnp.int32).reshape(1), weighted, near, far, squared, mask
-    )
+    y_block = line_len // n_vol
+    depth_corr = centred_sinc(jnp.arange(depth_len, dtype=jnp.int32), depth_len)
+    line_corr = centred_sinc(vol_index * y_block + jnp.arange(y_block, dtype=jnp.int32), line_len)
+    correction = line_corr[:, None] * depth_corr[None, :]
+    arrived = exchange(pieces, "vol")
+    arrived, weighted, squared, mask, correction = lax.optimization_barrier(
+        (arrived, weighted, squared, mask, correction)
+    )
+    mine = arrived.reshape(block, width)
+    near = gather_all(mine, "chip", n_chip).reshape(half, width)
+    far = swap(near)
+
+    send, keep, evidence = expect(scalars, weighted, near, far, squared, mask)
 
     rows = (keep.astype(f32) + swap(send).astype(f32)).astype(bf16)
     rows = scatter_sum(rows.reshape(n_chip, block, full), "chip")
@@ -353,17 +434,18 @@
     rows = gather_all(rows, "vol", n_vol).reshape(block, full)
     rows_near = gather_all(rows, "chip", n_chip).reshape(half, full)
     rows_far = swap(rows_near)
-    y_block = line_len // n_vol
-    lines = in_vmem(
-        lines_kernel, "lines", (n_vol, slab_depth, 2 * y_block),
-        mix_near, mix_far, rows_near, rows_far, *tables_line,
-    )
-    columns = exchange(lines, "vol").reshape(depth_len, 2 * y_block)
-    depth_corr = centred_sinc(jnp.arange(depth_len, dtype=jnp.int32), depth_len)
-    line_corr = centred_sinc(vol_index * y_block + jnp.arange(y_block, dtype=jnp.int32), line_len)
-    correction = line_corr[:, None] * depth_corr[None, :]
+    acc = in_vmem(
+        gather_kernel, "gather", jax.ShapeDtypeStruct((depth_len * per_line, full), f32),
+        (scalars,), place, rows_near,
+        cost=pl.CostEstimate(
+            flops=2 * depth_len * per_line * half * full,
+            bytes_accessed=4 * depth_len * per_line * full, transcendentals=0,
+        ),
+    )
     real_space = in_vmem(
-        depth_kernel, "depth", (2, y_block, depth_len), columns, correction, *tables_depth
+        finish_kernel, "finish", jax.ShapeDtypeStruct((2, y_block, depth_len), f32),
+        (scalars,), place, acc, rows_far, correction, *tables_line, *tables_depth,
+        scratch=(VMEM((2 * y_block, depth_len), f32),),
     )
     return (jnp.transpose(real_space, (0, 2, 1))[:, :, None, :], evidence[:, 0])
 

time: 184 us -> 190 us (1.033)
  blocking collectives: 117 us -> 70.7 us
  starting transfers between devices: 26.8 us -> 47.9 us
  Pallas kernels: 14.9 us -> 31.1 us
  local copies, waits for them, and re-layouts: 5.47 us -> 15 us
  waiting for transfers between devices: 14.1 us -> 19.5 us
    all_to_all x8 -> x5, blocking collectives: 117 us -> 70.7 us  [exchange(): return lax.all_to_all(pieces, axis, split_axis=0, concat_axis=0, tiled=True)]
    all_to_all x1 -> x3, starting transfers between devices: 3.85 us -> 25.5 us  [exchange(): return lax.all_to_all(pieces, axis, split_axis=0, concat_axis=0, tiled=True)]
    pallas_call x2 -> x3, Pallas kernels: 2.12 us -> 17.3 us  [in_vmem(): pl.pallas_call(kernel, out_shape=out_shape, in_specs=[pl.BlockSpec(memory...]
    unnamed x15 -> x21, local copies, waits for them, and re-layouts: 1.79 us -> 10.5 us
    all_to_all x1 -> x3, waiting for transfers between devices: 10.4 us -> 14.9 us  [exchange(): return lax.all_to_all(pieces, axis, split_axis=0, concat_axis=0, tiled=True)]
  transfers between devices with their start and end apart: 5 -> 7, of which waited for: 3 -> 5; matrix products, arithmetic and copies ran while one was open for 1% -> 1% of each run, Pallas kernels for 4% -> 11%
where the time goes in v1:
time: 190 us
  blocking collectives  70.7 us (37%)
  starting transfers between devices  47.9 us (25%)
  Pallas kernels  31.1 us (16%)
  waiting for transfers between devices  19.5 us (10%)
  local copies, waits for them, and re-layouts  15 us (8%)
  matrix products  2.53 us (1%)
    all_to_all x5, blocking collectives, exchange(): return lax.all_to_all(pieces, axis, split_axis=0, concat_axis=0, tiled=True)  70.7 us
    all_to_all x3, starting transfers between devices, exchange(): return lax.all_to_all(pieces, axis, split_axis=0, concat_axis=0, tiled=True)  25.5 us
    ppermute x4, starting transfers between devices, swap(): return lax.ppermute(value, 'core', [(0, 1), (1, 0)])  22.4 us
    pallas_call x3, Pallas kernels, in_vmem(): pl.pallas_call(kernel, out_shape=out_shape, in_specs=[pl.BlockSpec(memory...  17.3 us
    all_to_all x3, waiting for transfers between devices, exchange(): return lax.all_to_all(pieces, axis, split_axis=0, concat_axis=0, tiled=True)  14.9 us
    unnamed x21, local copies, waits for them, and re-layouts  10.5 us
    pallas_call x1, Pallas kernels, weigh(): pl.pallas_call(weighted_kernel, out_shape=jax.ShapeDtypeStruct((rows_per,...  5.61 us
    pallas_call x1, Pallas kernels, expect(): pl.pallas_call(expectation_kernel, out_shape=(half, half, jax.ShapeDtypeS...  5.59 us
  transfers between devices with their start and end apart: 7, of which 5 were waited for; matrix products, arithmetic and copies ran while one was open for 1% of the time, Pallas kernels for 11%

profile of v1, /device:TPU:1, one launch (start us, length us, event | category | flops | bytes accessed | tf_op | source)
XLA Modules:
  0.0 189.5 jit_solution(14216919927048522691)
XLA Ops:
  0.6 0.9 copy.28
  1.5 0.9 copy.26
  2.4 0.1 reshape.153
  2.4 0.9 copy.27
  3.3 0.1 reshape.154.factor_ref
  3.4 0.1 add_select_fusion.5
  3.6 0.2 select_reduce_fusion
  3.7 0.8 fusion.34
  4.6 8.7 %collective-permute-start = (f32[768,256]{1,0:T(8,128)S(1)}, f32[768,256]{1,0:T(8,128)S(1)}, u32[]{:S(2)}, u32[]{:S(2)}) collective-permute-start(f32[768,256]{1,0:T(8,128)S(1)} %fusion.34), channel_id=1, source_target_pairs={{0,32},{32,0},{1,33},{33,1},{2,34},{34,2},{3,35},{35,3},{4,36},{36... | collective-permute-start | bytes 2359304 | tf_op jit(solution)/shard_map/ppermute | solution.py:341
  13.3 0.2 select_reduce_fusion.1
  13.5 1.7 collective-permute-done
  15.2 1.7 convolution_add_fusion
  16.9 3.5 %all-to-all-start = ((f32[8,96,256]{2,1,0:T(8,128)}), f32[8,96,256]{2,1,0:T(8,128)S(1)}, u32[]{:S(2)}, u32[]{:S(2)}) async-start(f32[8,96,256]{2,1,0:T(8,128)} %bitcast.7), calls=%async_computation | async-start | bytes 1572864 | tf_op jit(solution)/shard_map/all_to_all | solution.py:329
  20.5 0.1 pad_add_fusion.order_ref.core_ref.place_scalar_ref
  20.6 12.5 %all-to-all-done = f32[8,96,256]{2,1,0:T(8,128)S(1)} async-done(((f32[8,96,256]{2,1,0:T(8,128)}), f32[8,96,256]{2,1,0:T(8,128)S(1)}, u32[]{:S(2)}, u32[]{:S(2)}) %all-to-all-start) | async-done | bytes 786464 | tf_op jit(solution)/shard_map/all_to_all | solution.py:329
  33.1 0.1 reduce_sum.56
  33.1 0.7 reshape.157
  33.8 10.4 %all-to-all-start.1 = ((f32[32,3,256]{2,1,0:T(4,128)}), f32[32,3,256]{2,1,0:T(4,128)S(1)}, u32[]{:S(2)}, u32[]{:S(2)}) async-start(f32[32,3,256]{2,1,0:T(4,128)} %reshape.157), calls=%async_computation.1 | async-start | bytes 262144 | tf_op jit(solution)/shard_map/all_to_all | solution.py:329
  44.2 0.1 broadcast_multiply_fusion.correction_ref
  44.3 2.6 %tables.1 = (bf16[512,512]{1,0:T(8,128)(2,1)S(1)}, bf16[512,512]{1,0:T(8,128)(2,1)S(1)}, bf16[512,512]{1,0:T(8,128)(2,1)S(1)}, bf16[512,512]{1,0:T(8,128)(2,1)S(1)}) custom-call(s32[2]{0:T(128)S(1)} %pad_add_fusion.order_ref.core_ref.place_scalar_ref), custom_call_target="tpu_custom_call" | custom-call | flops 7864320 | bytes 2097152 | tf_op jit(solution)/shard_map/tables/pallas_call | solution.py:298
  46.9 0.0 copy-start.7
  46.9 0.0 copy-start.8
  46.9 0.0 copy-start.9
  46.9 0.0 copy-start.4
  46.9 0.0 copy-start.5
  47.0 0.0 copy-start.6
  47.0 9.5 %placing.1.place_ref = bf16[2,2048,768]{2,1,0:T(8,128)(2,1)S(1)} custom-call(s32[8,1536]{1,0:T(8,128)S(1)} %get-tuple-element.36.index_ref, f32[8,1536]{1,0:T(8,128)S(1)} %reshape.154.factor_ref), custom_call_target="tpu_custom_call" | custom-call | flops 62914560 | bytes 6291456 | tf_op jit(solution)/shard_map/placing/pallas_call | solution.py:310
  56.5 0.0 copy-start
  56.5 2.6 %copy-done = bf16[2,2048,768]{2,1,0:T(8,128)(2,1)} copy-done((bf16[2,2048,768]{2,1,0:T(8,128)(2,1)}, bf16[2,2048,768]{2,1,0:T(8,128)(2,1)S(1)}, u32[]{:S(2)}) %copy-start) | copy-done | bytes 6291480
  59.2 0.0 all-to-all-done.1
  59.2 0.7 broadcast_in_dim.79
  59.9 11.6 %all-to-all-start.2 = ((bf16[32,3,256]{2,1,0:T(4,128)(2,1)}), bf16[32,3,256]{2,1,0:T(4,128)(2,1)S(1)}, u32[]{:S(2)}, u32[]{:S(2)}) async-start(bf16[32,3,256]{2,1,0:T(4,128)(2,1)} %broadcast_in_dim.79), calls=%async_computation.2 | async-start | bytes 131072 | tf_op jit(solution)/shard_map/all_to_all | solution.py:329
  71.5 0.0 copy-done.7
  71.5 0.3 copy.29
  71.8 0.0 copy-done.8
  71.8 0.1 fusion.9
  71.9 0.0 copy-done.5
  71.9 5.6 %weigh.1.weighted_ref = bf16[8,1024,256]{2,1,0:T(8,128)(2,1)S(1)} custom-call(bf16[32,8,256]{2,1,0:T(8,128)(2,1)S(1)} %copy-done.6, f32[32,8,128]{2,1,0:T(8,128)S(1)} %copy-done.4, f32[32,8,128]{2,1,0:T(8,128)S(1)} %copy-done.5, f32[1024,2]{1,0:T(8,128)S(1)} %bitcast.26), custom_call_target="tpu_custom_call" | custom-call | flops 83886080 | bytes 4194304 | tf_op jit(solution)/shard_map/weigh/pallas_call | solution.py:263
  77.5 2.0 %copy-done.2 = bf16[8,1024,256]{2,1,0:T(8,128)(2,1)} copy-done((bf16[8,1024,256]{2,1,0:T(8,128)(2,1)}, bf16[8,1024,256]{2,1,0:T(8,128)(2,1)S(1)}, u32[]{:S(2)}) %copy-start.2) | copy-done | bytes 4194328
  79.6 0.6 convert_reduce_fusion.mask_ref
  80.2 2.4 %all-to-all-done.2 = bf16[32,3,256]{2,1,0:T(4,128)(2,1)S(1)} async-done(((bf16[32,3,256]{2,1,0:T(4,128)(2,1)}), bf16[32,3,256]{2,1,0:T(4,128)(2,1)S(1)}, u32[]{:S(2)}, u32[]{:S(2)}) %all-to-all-start.2) | async-done | bytes 49184 | tf_op jit(solution)/shard_map/all_to_all | solution.py:329
  82.7 10.6 %all_to_all.40 = bf16[8,96,256]{2,1,0:T(8,128)(2,1)S(1)} all-to-all(bf16[8,96,256]{2,1,0:T(8,128)(2,1)S(1)} %broadcast_in_dim.82), channel_id=1, replica_groups=mesh['chip'=8,'core'=2,'vol'=32] {'chip'}, dimensions={0} | all-to-all | bytes 786432 | tf_op jit(solution)/shard_map/all_to_all | solution.py:329
  93.3 5.8 %collective-permute-start.1 = (bf16[768,256]{1,0:T(8,128)(2,1)S(1)}, bf16[768,256]{1,0:T(8,128)(2,1)S(1)}, u32[]{:S(2)}, u32[]{:S(2)}) collective-permute-start(bf16[768,256]{1,0:T(8,128)(2,1)S(1)} %bitcast.27), channel_id=1, source_target_pairs={{0,32},{32,0},{1,33},{33,1},{2,34},{34,2},{3,35},{35,3},{4,36},{36... | collective-permute-start | bytes 1179656 | tf_op jit(solution)/shard_map/ppermute | solution.py:341
  99.0 1.3 collective-permute-done.1.far_ref
  100.3 2.2 %copy-done.3 = bf16[8,1024,256]{2,1,0:T(8,128)(2,1)S(1)} copy-done((bf16[8,1024,256]{2,1,0:T(8,128)(2,1)S(1)}, bf16[8,1024,256]{2,1,0:T(8,128)(2,1)}, u32[]{:S(2)}) %copy-start.3) | copy-done | bytes 4194328
  102.5 5.6 %expect.1 = (bf16[768,384]{1,0:T(8,128)(2,1)S(1)}, bf16[768,384]{1,0:T(8,128)(2,1)S(1)}, f32[32,128]{1,0:T(8,128)S(1)}) custom-call(s32[2]{0:T(128)S(1)} %pad_add_fusion.order_ref.core_ref.place_scalar_ref, bf16[8,1024,256]{2,1,0:T(8,128)(2,1)S(1)} %copy-done.3, bf16[768,256]{1,0:T(8,128)(2,1)S(1)} %bitcast.28, ...), custom_call_target="tpu_custom_call" | custom-call | tf_op jit(solution)/shard_map/expect/pallas_call | solution.py:281
  108.1 2.3 %collective-permute-start.2 = (bf16[768,384]{1,0:T(8,128)(2,1)S(1)}, bf16[768,384]{1,0:T(8,128)(2,1)S(1)}, u32[]{:S(2)}, u32[]{:S(2)}) collective-permute-start(bf16[768,384]{1,0:T(8,128)(2,1)S(1)} %get-tuple-element.57), channel_id=1, source_target_pairs={{0,32},{32,0},{1,33},{33,1},{2,34},{34,2},{3,35},{35,3},{4,36},{36... | collective-permute-start | bytes 1769480 | tf_op jit(solution)/shard_map/ppermute | solution.py:341
  110.4 1.6 collective-permute-done.2
  112.0 0.2 add_convert_fusion
  112.2 12.8 %all_to_all.41 = bf16[8,96,384]{2,1,0:T(8,128)(2,1)S(1)} all-to-all(bf16[8,96,384]{2,1,0:T(8,128)(2,1)S(1)} %bitcast.29), channel_id=1, replica_groups=mesh['chip'=8,'core'=2,'vol'=32] {'chip'}, dimensions={0} | all-to-all | bytes 1179648 | tf_op jit(solution)/shard_map/all_to_all | solution.py:329
  125.0 0.1 convert_reduce_fusion.1
  125.1 0.1 reshape.161
  125.1 19.7 %all_to_all.42 = f32[32,3,384]{2,1,0:T(4,128)S(1)} all-to-all(f32[32,3,384]{2,1,0:T(4,128)S(1)} %reshape.161), channel_id=1, replica_groups=mesh['chip'=8,'core'=2,'vol'=32] {'vol'}, dimensions={0} | all-to-all | bytes 294912 | tf_op jit(solution)/shard_map/all_to_all | solution.py:329
  144.8 0.1 reduce_sum.59
  144.9 15.7 %all_to_all.43 = bf16[32,3,384]{2,1,0:T(4,128)(2,1)S(1)} all-to-all(bf16[32,3,384]{2,1,0:T(4,128)(2,1)S(1)} %broadcast_in_dim.83), channel_id=1, replica_groups=mesh['chip'=8,'core'=2,'vol'=32] {'vol'}, dimensions={0} | all-to-all | bytes 147456 | tf_op jit(solution)/shard_map/all_to_all | solution.py:329
  160.6 0.1 broadcast_in_dim.84
  160.6 0.1 broadcast_in_dim.85
  160.7 12.0 %all_to_all.44 = bf16[8,96,384]{2,1,0:T(8,128)(2,1)S(1)} all-to-all(bf16[8,96,384]{2,1,0:T(8,128)(2,1)S(1)} %broadcast_in_dim.85), channel_id=1, replica_groups=mesh['chip'=8,'core'=2,'vol'=32] {'chip'}, dimensions={0} | all-to-all | bytes 1179648 | tf_op jit(solution)/shard_map/all_to_all | solution.py:329
  172.7 5.6 %collective-permute-start.3 = (bf16[768,384]{1,0:T(8,128)(2,1)S(1)}, bf16[768,384]{1,0:T(8,128)(2,1)S(1)}, u32[]{:S(2)}, u32[]{:S(2)}) collective-permute-start(bf16[768,384]{1,0:T(8,128)(2,1)S(1)} %bitcast.24), channel_id=1, source_target_pairs={{0,32},{32,0},{1,33},{33,1},{2,34},{34,2},{3,35},{35,3},{4,36},{36... | collective-permute-start | bytes 1769480 | tf_op jit(solution)/shard_map/ppermute | solution.py:341
  178.3 0.6 slice_reduce_fusion
  178.9 2.8 %copy-done.1 = bf16[2,2048,768]{2,1,0:T(8,128)(2,1)S(1)} copy-done((bf16[2,2048,768]{2,1,0:T(8,128)(2,1)S(1)}, bf16[2,2048,768]{2,1,0:T(8,128)(2,1)}, u32[]{:S(2)}) %copy-start.1) | copy-done | bytes 6291480
  181.7 2.4 %gather.1.acc_ref = f32[2048,384]{1,0:T(8,128)S(1)} custom-call(s32[2]{0:T(128)S(1)} %pad_add_fusion.order_ref.core_ref.place_scalar_ref, bf16[2,2048,768]{2,1,0:T(8,128)(2,1)S(1)} %copy-done.1, bf16[768,384]{1,0:T(8,128)(2,1)S(1)} %bitcast.25), custom_call_target="tpu_custom_call" | custom-call | flops 1207959552 | bytes 3145728 | tf_op jit(solution)/shard_map/gather/pallas_call | solution.py:310
  184.1 0.0 collective-permute-done.3.rows_ref
  184.1 5.4 %finish.1 = f32[2,16,512]{2,1,0:T(8,128)} custom-call(s32[2]{0:T(128)S(1)} %pad_add_fusion.order_ref.core_ref.place_scalar_ref, bf16[2,2048,768]{2,1,0:T(8,128)(2,1)S(1)} %copy-done.1, f32[2048,384]{1,0:T(8,128)S(1)} %gather.1.acc_ref, bf16[768,384]{1,0:T(8,128)(2,1)S(1)} %collective-permute-done.3.rows_ref, ...), custom_call_target="tpu_custom_call" | custom-call | tf_op jit(solution)/shard_map/finish/pallas_call | solution.py:310
  (15 shorter events, 0.3 us)
Async XLA Ops:
  4.6 10.6 %collective-permute-start = (f32[768,256]{1,0:T(8,128)S(1)}, f32[768,256]{1,0:T(8,128)S(1)}, u32[]{:S(2)}, u32[]{:S(2)}) collective-permute-start(f32[768,256]{1,0:T(8,128)S(1)} %fusion.34), channel_id=1, source_target_pairs={{0,32},{32,0},{1,33},{33,1},{2,34},{34,2},{3,35},{35,3},{4,36},{36... | collective-permute-start | bytes 2359304 | tf_op jit(solution)/shard_map/ppermute | solution.py:341
  16.9 16.1 %all-to-all-start = ((f32[8,96,256]{2,1,0:T(8,128)}), f32[8,96,256]{2,1,0:T(8,128)S(1)}, u32[]{:S(2)}, u32[]{:S(2)}) async-start(f32[8,96,256]{2,1,0:T(8,128)} %bitcast.7), calls=%async_computation | async-start | bytes 1572864 | tf_op jit(solution)/shard_map/all_to_all | solution.py:329
  33.8 25.3 %all-to-all-start.1 = ((f32[32,3,256]{2,1,0:T(4,128)}), f32[32,3,256]{2,1,0:T(4,128)S(1)}, u32[]{:S(2)}, u32[]{:S(2)}) async-start(f32[32,3,256]{2,1,0:T(4,128)} %reshape.157), calls=%async_computation.1 | async-start | bytes 262144 | tf_op jit(solution)/shard_map/all_to_all | solution.py:329
  46.9 24.6 %copy-start.7 = (f32[32,2,32]{2,1,0:T(2,128)S(1)}, f32[32,2,32]{2,1,0:T(2,128)}, u32[]{:S(2)}) copy-start(f32[32,2,32]{2,1,0:T(2,128)} %param.13) | copy-start | bytes 24580
  46.9 24.9 %copy-start.8 = (s32[32,64]{1,0:T(8,128)S(1)}, s32[32,64]{1,0:T(8,128)}, u32[]{:S(2)}) copy-start(s32[32,64]{1,0:T(8,128)} %param.14) | copy-start | bytes 24580
  46.9 24.9 %copy-start.9 = (s32[32]{0:T(128)S(1)}, s32[32]{0:T(128)}, u32[]{:S(2)}) copy-start(s32[32]{0:T(128)} %param.15) | copy-start | bytes 388
  46.9 24.9 %copy-start.4 = (f32[32,8,128]{2,1,0:T(8,128)S(1)}, f32[32,8,128]{2,1,0:T(8,128)}, u32[]{:S(2)}) copy-start(f32[32,8,128]{2,1,0:T(8,128)} %ctf_ref) | copy-start | bytes 393220
  46.9 24.9 %copy-start.5 = (f32[32,8,128]{2,1,0:T(8,128)S(1)}, f32[32,8,128]{2,1,0:T(8,128)}, u32[]{:S(2)}) copy-start(f32[32,8,128]{2,1,0:T(8,128)} %noise_ref) | copy-start | bytes 393220
  47.0 25.0 %copy-start.6 = (bf16[32,8,256]{2,1,0:T(8,128)(2,1)S(1)}, bf16[32,8,256]{2,1,0:T(8,128)(2,1)}, u32[]{:S(2)}) copy-start(bf16[32,8,256]{2,1,0:T(8,128)(2,1)} %images_ref) | copy-start | bytes 393220
  56.5 2.7 %copy-start = (bf16[2,2048,768]{2,1,0:T(8,128)(2,1)}, bf16[2,2048,768]{2,1,0:T(8,128)(2,1)S(1)}, u32[]{:S(2)}) copy-start(bf16[2,2048,768]{2,1,0:T(8,128)(2,1)S(1)} %placing.1.place_ref) | copy-start | bytes 18874372
  59.9 22.7 %all-to-all-start.2 = ((bf16[32,3,256]{2,1,0:T(4,128)(2,1)}), bf16[32,3,256]{2,1,0:T(4,128)(2,1)S(1)}, u32[]{:S(2)}, u32[]{:S(2)}) async-start(bf16[32,3,256]{2,1,0:T(4,128)(2,1)} %broadcast_in_dim.79), calls=%async_computation.2 | async-start | bytes 131072 | tf_op jit(solution)/shard_map/all_to_all | solution.py:329
  77.5 2.0 %copy-start.2 = (bf16[8,1024,256]{2,1,0:T(8,128)(2,1)}, bf16[8,1024,256]{2,1,0:T(8,128)(2,1)S(1)}, u32[]{:S(2)}) copy-start(bf16[8,1024,256]{2,1,0:T(8,128)(2,1)S(1)} %weigh.1.weighted_ref) | copy-start | bytes 12582916
  93.3 7.1 %collective-permute-start.1 = (bf16[768,256]{1,0:T(8,128)(2,1)S(1)}, bf16[768,256]{1,0:T(8,128)(2,1)S(1)}, u32[]{:S(2)}, u32[]{:S(2)}) collective-permute-start(bf16[768,256]{1,0:T(8,128)(2,1)S(1)} %bitcast.27), channel_id=1, source_target_pairs={{0,32},{32,0},{1,33},{33,1},{2,34},{34,2},{3,35},{35,3},{4,36},{36... | collective-permute-start | bytes 1179656 | tf_op jit(solution)/shard_map/ppermute | solution.py:341
  100.3 2.2 %copy-start.3 = (bf16[8,1024,256]{2,1,0:T(8,128)(2,1)S(1)}, bf16[8,1024,256]{2,1,0:T(8,128)(2,1)}, u32[]{:S(2)}) copy-start(bf16[8,1024,256]{2,1,0:T(8,128)(2,1)} %copy-done.2) | copy-start | bytes 12582916
  108.1 3.9 %collective-permute-start.2 = (bf16[768,384]{1,0:T(8,128)(2,1)S(1)}, bf16[768,384]{1,0:T(8,128)(2,1)S(1)}, u32[]{:S(2)}, u32[]{:S(2)}) collective-permute-start(bf16[768,384]{1,0:T(8,128)(2,1)S(1)} %get-tuple-element.57), channel_id=1, source_target_pairs={{0,32},{32,0},{1,33},{33,1},{2,34},{34,2},{3,35},{35,3},{4,36},{36... | collective-permute-start | bytes 1769480 | tf_op jit(solution)/shard_map/ppermute | solution.py:341
  172.7 11.4 %collective-permute-start.3 = (bf16[768,384]{1,0:T(8,128)(2,1)S(1)}, bf16[768,384]{1,0:T(8,128)(2,1)S(1)}, u32[]{:S(2)}, u32[]{:S(2)}) collective-permute-start(bf16[768,384]{1,0:T(8,128)(2,1)S(1)} %bitcast.24), channel_id=1, source_target_pairs={{0,32},{32,0},{1,33},{33,1},{2,34},{34,2},{3,35},{35,3},{4,36},{36... | collective-permute-start | bytes 1769480 | tf_op jit(solution)/shard_map/ppermute | solution.py:341
  178.9 2.8 %copy-start.1 = (bf16[2,2048,768]{2,1,0:T(8,128)(2,1)S(1)}, bf16[2,2048,768]{2,1,0:T(8,128)(2,1)}, u32[]{:S(2)}) copy-start(bf16[2,2048,768]{2,1,0:T(8,128)(2,1)} %copy-done) | copy-start | bytes 18874372
